TPU v7x, 256 devices: a whole 4x4x8 slice. The times are simulated.
256 devices in a mesh: song: 4 (over y), seq: 64 (over z, x, core).
Axes of the slice: x: 4, y: 4, z: 8, core: 2. Of those that a mesh axis runs over, the one named last changes fastest.
Arguments:
- queries: bfloat16 [4, 8192, 2048], P('song', 'seq'), may hold values from -64 to 64
- keys: bfloat16 [4, 8192, 2048], P('song', 'seq'), may hold values from -64 to 64
- values: bfloat16 [4, 8192, 2048], P('song', 'seq'), may hold values from -6 to 6
- lyric_keys: bfloat16 [4, 384, 2048], P('song', 'seq'), may hold values from -64 to 64
- lyric_values: bfloat16 [4, 384, 2048], P('song', 'seq'), may hold values from -6 to 6
- q_gain: float32 [128], replicated, may hold values from 0.5 to 1.5
- k_gain: float32 [128], replicated, may hold values from 0.5 to 1.5
- cotangent: bfloat16 [4, 8192, 2048], P('song', 'seq'), may hold values from -12 to 12
- alignment: int32 [4, 64, 2], P('song', 'seq'), may hold values from -1 to 2, as said below
- lyric_len: int32 [4], P('song'), may hold values from 192 to 384
Outputs:
- attn_out: bfloat16 [4, 8192, 2048], P('song', 'seq')
- grad_queries: bfloat16 [4, 8192, 2048], P('song', 'seq')
- grad_keys: bfloat16 [4, 8192, 2048], P('song', 'seq')
- grad_values: bfloat16 [4, 8192, 2048], P('song', 'seq')
- grad_lyric_keys: bfloat16 [4, 384, 2048], P('song', 'seq')
- grad_lyric_values: bfloat16 [4, 384, 2048], P('song', 'seq')
- grad_q_gain: float32 [128], replicated
- grad_k_gain: float32 [128], replicated
Inputs may be any that keep to these rules, and one draw needn't show every extreme that they name: `alignment`: in each row the entries that are not -1 are distinct.
All inputs are finite; a program needn't handle non-finite values.
Results may differ from a plain program's by a relative error of at most 0.01.
Values may be sent and summed in bfloat16 or wider, within the bound.
A program may use at most 128 MiB of HBM per device.

v0:
```python
import jax
import jax.numpy as jnp
from jax import lax
from jax.sharding import PartitionSpec as P

BLK = 128
WIN = 1
TILES = 2
NORM_EPS = 1e-06


def extended_2(block, sides, width):
    for axis, dim in sides:
        count = lax.axis_size(axis)
        forward = [(i, i + 1) for i in range(count - 1)]
        backward = [(target, source) for source, target in forward]
        low = lax.ppermute(
            lax.slice_in_dim(block, block.shape[dim] - width, None, axis=dim), axis, forward
        )
        high = lax.ppermute(lax.slice_in_dim(block, 0, width, axis=dim), axis, backward)
        block = jnp.concatenate([low, block, high], axis=dim)
    return block


def norm_heads(inputs, norm_gain):
    row_values = inputs.astype(jnp.float32).reshape(inputs.shape[0], -1, norm_gain.shape[0])
    inverse = lax.rsqrt(jnp.mean(row_values * row_values, axis=-1, keepdims=True) + NORM_EPS)
    return (row_values * inverse * norm_gain, inverse)


def norm_back(inputs, inverse, norm_gain, grad_out):
    row_values = inputs.astype(jnp.float32).reshape(grad_out.shape)
    scaled = grad_out * norm_gain
    grad_input = inverse * scaled - row_values * inverse * inverse * inverse * jnp.mean(
        scaled * row_values, axis=-1, keepdims=True
    )
    grad_gain = jnp.sum(grad_out * row_values * inverse, axis=(0, 1))
    return (grad_input.reshape(inputs.shape), grad_gain)


def block_pass(query_rows, key_rows, value_rows, keep_mask, grad_rows, score_scale):
    scores = (
        jnp.einsum("qhd,khd->hqk", query_rows, key_rows, preferred_element_type=jnp.float32)
        * score_scale
    )
    exp_scores = jnp.where(keep_mask[None, None, :], jnp.exp(scores), 0.0)
    totals = jnp.sum(exp_scores, axis=2)
    prob_full = exp_scores / totals[:, :, None]
    prob_low = prob_full.astype(jnp.bfloat16)
    block_output = jnp.einsum(
        "hqk,khd->qhd", prob_low, value_rows, preferred_element_type=jnp.float32
    ).astype(jnp.bfloat16)
    delta_rows = jnp.sum(grad_rows.astype(jnp.float32) * block_output.astype(jnp.float32), axis=2).T
    grad_prob = jnp.einsum(
        "qhd,khd->hqk", grad_rows, value_rows, preferred_element_type=jnp.float32
    )
    grad_score = (prob_full * (grad_prob - delta_rows[:, :, None])).astype(jnp.bfloat16)
    query_gradient = (
        jnp.einsum("hqk,khd->qhd", grad_score, key_rows, preferred_element_type=jnp.float32)
        * score_scale
    )
    grad_key = (
        jnp.einsum("hqk,qhd->khd", grad_score, query_rows, preferred_element_type=jnp.float32)
        * score_scale
    )
    value_gradient = jnp.einsum(
        "hqk,qhd->khd", prob_low, grad_rows, preferred_element_type=jnp.float32
    )
    return (block_output, query_gradient, grad_key, value_gradient, totals, delta_rows)


def body(
    queries, keys, values, lyric_keys, lyric_values, q_gain, k_gain, cotangent, alignment, lyric_len
):
    head_size = q_gain.shape[0]
    model_width = queries.shape[2]
    head_count = model_width // head_size
    frames = queries.shape[1]
    lyric_local = lyric_keys.shape[1]
    blocks = frames // BLK
    border_rows = WIN * BLK
    window_extent = (2 * WIN + 1) * BLK
    score_scale = head_size ** (-0.5)
    total_frames = frames * lax.axis_size("seq")
    first_frame = lax.axis_index("seq") * frames
    query_raw = queries[0]
    key_raw = keys[0]
    query_full, query_inv = norm_heads(query_raw, q_gain)
    key_full, key_inv = norm_heads(key_raw, k_gain)
    lyric_full, lyric_inv = norm_heads(lyric_keys[0], k_gain)
    query_norm = query_full.astype(jnp.bfloat16)
    key_norm = key_full.astype(jnp.bfloat16)
    lyric_norm = lyric_full.astype(jnp.bfloat16)
    lyric_key_all, lyric_val_all = (
        lax.all_gather(lyric_norm.reshape(lyric_local, model_width), "seq", axis=0, tiled=True),
        lax.all_gather(lyric_values[0], "seq", axis=0, tiled=True),
    )
    lyric_total = lyric_key_all.shape[0]
    lyric_key_all = lyric_key_all.reshape(lyric_total, head_count, head_size)
    lyric_val_all = lyric_val_all.reshape(lyric_total, head_count, head_size)
    stacked = jnp.stack([key_norm.reshape(frames, model_width), values[0]])
    extended = extended_2(stacked, (("seq", 1),), border_rows)
    ext_keys = extended[0].reshape(frames + 2 * border_rows, head_count, head_size)
    ext_vals = extended[1].reshape(frames + 2 * border_rows, head_count, head_size)
    grad_heads = cotangent[0].reshape(frames, head_count, head_size)
    length = lyric_len[0]

    def one_block(block_id):
        start_offset = block_id * BLK
        position = (
            first_frame + start_offset - border_rows + jnp.arange(window_extent, dtype=jnp.int32)
        )
        audio_mask = (position >= 0) & (position < total_frames)
        tile_ids = alignment[0, block_id]
        row_grid = (jnp.maximum(tile_ids, 0) * BLK)[:, None] + jnp.arange(BLK, dtype=jnp.int32)[
            None, :
        ]
        lyric_mask = ((tile_ids >= 0)[:, None] & (row_grid < length)).reshape(-1)
        row_index = row_grid.reshape(-1)
        all_keys = jnp.concatenate([ext_keys, jnp.take(lyric_key_all, row_index, axis=0)], axis=0)
        all_vals = jnp.concatenate([ext_vals, jnp.take(lyric_val_all, row_index, axis=0)], axis=0)
        keep_mask = jnp.concatenate([audio_mask, lyric_mask], axis=0)
        results = block_pass(query_norm, all_keys, all_vals, keep_mask, grad_heads, score_scale)
        return results + (row_index,)

    output_list, grad_qn, grad_key, value_gradient, totals, delta_rows, row_index = lax.map(
        one_block, jnp.arange(blocks, dtype=jnp.int32)
    )
    audio_cols = grad_key.shape[1] - TILES * BLK
    flat_rows = row_index.reshape(-1)
    lyric_grad_key = (
        jnp.zeros((lyric_total, head_count, head_size), jnp.float32)
        .at[flat_rows]
        .add(grad_key[:, audio_cols:].reshape(-1, head_count, head_size))
    )
    lyric_grad_val = (
        jnp.zeros((lyric_total, head_count, head_size), jnp.float32)
        .at[flat_rows]
        .add(value_gradient[:, audio_cols:].reshape(-1, head_count, head_size))
    )
    ext_grad_key = jnp.zeros((frames + 2 * border_rows, head_count, head_size), jnp.float32)
    ext_grad_val = jnp.zeros((frames + 2 * border_rows, head_count, head_size), jnp.float32)
    block_id = 0
    lower = block_id * BLK
    ext_grad_key = ext_grad_key.at[lower : lower + window_extent].add(
        grad_key[block_id, :window_extent]
    )
    ext_grad_val = ext_grad_val.at[lower : lower + window_extent].add(
        value_gradient[block_id, :window_extent]
    )
    own_grad_key = ext_grad_key[border_rows : border_rows + frames]
    own_grad_val = ext_grad_val[border_rows : border_rows + frames]
    rims = jnp.stack(
        [
            jnp.concatenate(
                [ext_grad_key[:border_rows], ext_grad_key[border_rows + frames :]], axis=0
            ).reshape(2 * border_rows, model_width),
            jnp.concatenate(
                [ext_grad_val[:border_rows], ext_grad_val[border_rows + frames :]], axis=0
            ).reshape(2 * border_rows, model_width),
        ]
    )
    received = extended_2(rims.astype(jnp.bfloat16), (("seq", 1),), border_rows).astype(rims.dtype)
    from_left = received[:, :border_rows].reshape(2, border_rows, head_count, head_size)
    from_right = received[:, 3 * border_rows :].reshape(2, border_rows, head_count, head_size)
    own_grad_key = (
        own_grad_key.at[:border_rows]
        .add(from_left[0])
        .at[frames - border_rows :]
        .add(from_right[0])
    )
    own_grad_val = (
        own_grad_val.at[:border_rows]
        .add(from_left[1])
        .at[frames - border_rows :]
        .add(from_right[1])
    )
    unnormed_query_gradient, query_gain_vector = norm_back(
        query_raw, query_inv, q_gain, grad_qn.reshape(frames, head_count, head_size)
    )
    unnormed_key_gradient, key_gain_vector = norm_back(key_raw, key_inv, k_gain, own_grad_key)
    summed_key, summed_val = (
        lax.psum_scatter(
            lyric_grad_key.reshape(lyric_total, model_width), "seq", scatter_dimension=0, tiled=True
        ),
        lax.psum_scatter(
            lyric_grad_val.reshape(lyric_total, model_width), "seq", scatter_dimension=0, tiled=True
        ),
    )
    unnormed_lyric_gradient, lyric_gain_vector = norm_back(
        lyric_keys[0], lyric_inv, k_gain, summed_key.reshape(lyric_local, head_count, head_size)
    )
    total_query_gain, total_key_gain = lax.psum(
        (query_gain_vector, key_gain_vector + lyric_gain_vector), ("song", "seq")
    )
    return (
        output_list.reshape(1, frames, model_width),
        unnormed_query_gradient.astype(jnp.bfloat16)[None],
        unnormed_key_gradient.astype(jnp.bfloat16)[None],
        own_grad_val.reshape(1, frames, model_width).astype(jnp.bfloat16),
        unnormed_lyric_gradient.astype(jnp.bfloat16)[None],
        summed_val.astype(jnp.bfloat16)[None],
        total_query_gain,
        total_key_gain,
    )


def solution(mesh):
    in_specs = (
        P("song", "seq", None),
        P("song", "seq", None),
        P("song", "seq", None),
        P("song", "seq", None),
        P("song", "seq", None),
        P(),
        P(),
        P("song", "seq", None),
        P("song", "seq", None),
        P("song"),
    )
    out_specs = (
        P("song", "seq", None),
        P("song", "seq", None),
        P("song", "seq", None),
        P("song", "seq", None),
        P("song", "seq", None),
        P("song", "seq", None),
        P(),
        P(),
    )
    return jax.shard_map(body, mesh=mesh, in_specs=in_specs, out_specs=out_specs, check_vma=False)
```

profile of v0, /device:TPU:1, one launch (start us, length us, event | category | flops | bytes accessed | tf_op | source)
XLA Modules:
  0.0 654.3 jit_solution(4677205366677550377)
XLA Ops:
  16.2 5.2 collective-permute-start.1
  27.9 5.7 collective-permute-done.1
  40.4 53.5 %all-gather.5.cloned.1.call-done = bf16[1,384,2048]{2,0,1:T(2,128)(2,1)} async-done(((bf16[1,6,2048]{2,0,1:T(2,128)(2,1)}), bf16[1,384,2048]{2,0,1:T(2,128)(2,1)}) %all-gather.5.cloned.1.call-update) | async-done | bytes 1572880 | tf_op jit(solution)/shard_map/all_gather | solution.py:96
  93.9 6.9 %copy.100 = bf16[1,384,2048]{1,2,0:T(8,128)(2,1)S(1)} copy(bf16[1,384,2048]{2,0,1:T(2,128)(2,1)} %all-gather.5.cloned.1.call-done) | data formatting | bytes 3145728 | tf_op jit(solution)/shard_map/all_gather | solution.py:96
  102.9 69.1 %all-gather.7.cloned.1.call-done = bf16[64,6,2048]{2,1,0:T(8,128)(2,1)} async-done(((bf16[1,6,2048]{2,1,0:T(8,128)(2,1)}), bf16[64,6,2048]{2,1,0:T(8,128)(2,1)}) %all-gather.7.cloned.1.call-update) | async-done | bytes 1572880 | tf_op jit(solution)/shard_map/all_gather | solution.py:95
  172.0 4.4 reshape.472
  176.4 3.2 gather_fusion.1
  186.3 3.1 fusion.56
  189.5 2.4 multiply_reduce_fusion
  196.8 2.1 fusion.55
  198.9 2.1 collective-permute-start.3
  201.0 3.6 collective-permute-start.2
  207.0 20.2 %scatter_fusion = f32[384,16,128]{2,1,0:T(8,128)S(1)} fusion(f32[384,16,128]{2,1,0:T(8,128)S(1)} %broadcast.403.clone, s32[256]{0:T(256)S(1)} %bitcast.227, f32[256,16,128]{2,1,0:T(8,128)} %copy.112), kind=kCustom, calls=%fused_computation.2 | custom fusion | flops 524288 | bytes 6292480 | tf_op jit(solution)/shard_map/scatter-add | solution.py:134
  227.3 3.1 copy.146
  234.4 20.2 %scatter_fusion.1 = f32[384,16,128]{2,1,0:T(8,128)S(1)} fusion(f32[384,16,128]{2,1,0:T(8,128)S(1)} %broadcast.403.clone.1, s32[256]{0:T(256)S(1)} %bitcast.228, f32[256,16,128]{2,1,0:T(8,128)} %copy.113), kind=kCustom, calls=%fused_computation.3 | custom fusion | flops 524288 | bytes 6292480 | tf_op jit(solution)/shard_map/scatter-add | solution.py:139
  254.6 3.1 copy.145
  257.7 279.7 %all-reduce.7 = bf16[384,2048]{1,0:T(8,128)(2,1)} all-reduce(f32[384,2048]{1,0:T(8,128)} %bitcast.203), channel_id=4, replica_groups=mesh['song'=4,'seq'=64] {'seq'}, use_global_device_ids=true, to_apply=%region_11.13.clone | all-reduce | flops 786432 | bytes 4718592
  537.4 4.1 fusion.18
  542.9 2.4 slice.228
  545.3 2.0 copy.114
  547.4 2.3 fusion.25
  549.7 2.0 copy.115
  557.9 2.0 copy.116
  565.4 82.4 %all-reduce.2 = (f32[128]{0:T(128)}, f32[128]{0:T(128)}) all-reduce(f32[128]{0:T(128)S(1)} %get-tuple-element.214, f32[128]{0:T(128)S(1)} %add.202), channel_id=1, replica_groups=mesh['song'=4,'seq'=64] {'song','seq'}, use_global_device_ids=true, to_apply=%region_13.15 | all-reduce | flops 256 | bytes 2048 | tf_op jit(solution)/shard_map/psum | solution.py:193
  (126 shorter events, 53.6 us)
Async XLA Ops:
  7.2 86.8 %all-gather.5.cloned.1.call-start = ((), (), s32[]{:S(2)}) async-start(), calls=%async_computation | async-start | bytes 3194880 | tf_op jit(solution)/shard_map/all_gather | solution.py:96
  8.7 163.3 %all-gather.7.cloned.1.call-start = ((), (), s32[]{:S(2)}) async-start(), calls=%async_computation.1 | async-start | bytes 2129920 | tf_op jit(solution)/shard_map/all_gather | solution.py:95
  11.7 550.9 %all-reduce.6.cloned.1.call-start = ((), (), s32[]{:S(2)}) async-start(), calls=%async_computation.2 | async-start | bytes 6291456
  13.1 10.9 %copy-start.24 = (s32[1,1,2]{2,1,0:T(1,128)S(1)}, s32[1,1,2]{2,1,0:T(1,128)}, u32[]{:S(2)}) copy-start(s32[1,1,2]{2,1,0:T(1,128)} %param.44) | copy-start | bytes 28
  13.1 11.0 %copy-start.19 = (bf16[1,128,2048]{2,1,0:T(8,128)(2,1)S(1)}, bf16[1,128,2048]{2,1,0:T(8,128)(2,1)}, u32[]{:S(2)}) copy-start(bf16[1,128,2048]{2,1,0:T(8,128)(2,1)} %param.43) | copy-start | bytes 1572868
  14.5 9.6 %copy-start.3 = (bf16[1,128,2048]{1,2,0:T(8,128)(2,1)}, bf16[1,128,2048]{1,2,0:T(8,128)(2,1)S(1)}, u32[]{:S(2)}) copy-start(bf16[1,128,2048]{1,2,0:T(8,128)(2,1)S(1)} %copy.97) | copy-start | bytes 1572868
  15.7 10.7 %copy-start.25 = (u32[256]{0:T(256)S(1)}, u32[256]{0:T(256)}, u32[]{:S(2)}) copy-start(u32[256]{0:T(256)} %constant.274) | copy-start | bytes 3076
  16.1 11.7 %copy-start.23 = (f32[128]{0:T(128)S(1)}, f32[128]{0:T(128)}, u32[]{:S(2)}) copy-start(f32[128]{0:T(128)} %param.41) | copy-start | bytes 1540
  16.2 17.4 %collective-permute-start.1 = (bf16[2,128,2048]{1,2,0:T(8,128)(2,1)S(1)}, bf16[2,128,2048]{1,2,0:T(8,128)(2,1)}, u32[]{:S(2)}, u32[]{:S(2)}) collective-permute-start(bf16[2,128,2048]{1,2,0:T(8,128)(2,1)S(1)} %pad_maximum_fusion.9), channel_id=1, source_target_pairs={{1,0},{2,1},{3,2},{4,3},{5,4},{6,5},{7,6},{8,7},{9,8},{10,9},{11,1... | collective-permute-start | bytes 3145736 | tf_op jit(solution)/shard_map/ppermute | solution.py:20
  21.4 14.2 %collective-permute-start = (bf16[2,128,2048]{1,2,0:T(8,128)(2,1)S(1)}, bf16[2,128,2048]{1,2,0:T(8,128)(2,1)}, u32[]{:S(2)}, u32[]{:S(2)}) collective-permute-start(bf16[2,128,2048]{1,2,0:T(8,128)(2,1)S(1)} %pad_maximum_fusion.9), channel_id=1, source_target_pairs={{0,1},{1,2},{2,3},{3,4},{4,5},{5,6},{6,7},{7,8},{8,9},{9,10},{10,1... | collective-permute-start | bytes 3145736 | tf_op jit(solution)/shard_map/ppermute | solution.py:17
  26.4 167.4 %copy-start.1 = (f32[1,128,2048]{1,2,0:T(8,128)}, f32[1,128,2048]{1,2,0:T(8,128)S(1)}, u32[]{:S(2)}) copy-start(f32[1,128,2048]{1,2,0:T(8,128)S(1)} %copy.103) | copy-start | bytes 3145732
  102.9 76.7 %copy-start.12 = (bf16[384,16,128]{2,1,0:T(8,128)(2,1)S(1)}, bf16[384,16,128]{2,1,0:T(8,128)(2,1)}, u32[]{:S(2)}) copy-start(bf16[384,16,128]{2,1,0:T(8,128)(2,1)} %copy.101) | copy-start | bytes 4718596
  186.3 3.1 copy-start.17
  195.3 9.4 %copy-start = (f32[1,640,16,128]{1,3,2,0:T(8,128)}, f32[1,640,16,128]{1,3,2,0:T(8,128)S(1)}, u32[]{:S(2)}) copy-start(f32[1,640,16,128]{1,3,2,0:T(8,128)S(1)} %get-tuple-element.244) | copy-start | bytes 15728644
  195.8 3.1 copy-start.9
  198.9 354.3 %collective-permute-start.3 = (bf16[2,128,2048]{1,2,0:T(8,128)(2,1)}, bf16[2,128,2048]{1,2,0:T(8,128)(2,1)}, u32[]{:S(2)}, u32[]{:S(2)}) collective-permute-start(bf16[2,128,2048]{1,2,0:T(8,128)(2,1)} %get-tuple-element.234), channel_id=1, source_target_pairs={{1,0},{2,1},{3,2},{4,3},{5,4},{6,5},{7,6},{8,7},{9,8},{10,9},{11,1... | collective-permute-start | bytes 3145736 | tf_op jit(solution)/shard_map/ppermute | solution.py:20
  201.0 352.2 %collective-permute-start.2 = (bf16[2,128,2048]{1,2,0:T(8,128)(2,1)}, bf16[2,128,2048]{1,2,0:T(8,128)(2,1)}, u32[]{:S(2)}, u32[]{:S(2)}) collective-permute-start(bf16[2,128,2048]{1,2,0:T(8,128)(2,1)} %get-tuple-element.233), channel_id=1, source_target_pairs={{0,1},{1,2},{2,3},{3,4},{4,5},{5,6},{6,7},{7,8},{8,9},{9,10},{10,1... | collective-permute-start | bytes 3145736 | tf_op jit(solution)/shard_map/ppermute | solution.py:17
  257.7 279.7 %copy-start.2 = (f32[1,128,2048]{1,2,0:T(8,128)S(1)}, f32[1,128,2048]{1,2,0:T(8,128)}, u32[]{:S(2)}) copy-start(f32[1,128,2048]{1,2,0:T(8,128)} %copy-done.1) | copy-start | bytes 3145732
  257.7 279.7 %copy-start.16 = (bf16[384,16,128]{2,0,1:T(8,128)(2,1)S(1)}, bf16[384,16,128]{2,0,1:T(8,128)(2,1)}, u32[]{:S(2)}) copy-start(bf16[384,16,128]{2,0,1:T(8,128)(2,1)} %copy.105) | copy-start | bytes 4718596
  542.9 10.3 %copy-start.4 = (bf16[1,128,2048]{1,2,0:T(8,128)(2,1)S(1)}, bf16[1,128,2048]{1,2,0:T(8,128)(2,1)}, u32[]{:S(2)}) copy-start(bf16[1,128,2048]{1,2,0:T(8,128)(2,1)} %copy-done.3) | copy-start | bytes 1572868
  542.9 10.3 %copy-start.6 = (bf16[1,128,16,128]{1,3,2,0:T(8,128)(2,1)S(1)}, bf16[1,128,16,128]{1,3,2,0:T(8,128)(2,1)}, u32[]{:S(2)}) copy-start(bf16[1,128,16,128]{1,3,2,0:T(8,128)(2,1)} %copy-done.5) | copy-start | bytes 1572868
  556.6 3.3 copy-start.8
  556.6 3.3 copy-start.10
  559.9 3.8 copy-start.21
  (9 other events, 15.5 us)
Sparse Core Ops, SparseCore 0:
  11.3 82.5 all-gather.4
  97.3 74.6 all-gather.6
  230.5 192.0 all-reduce.5
where the time goes:
time: 656 us; the launch traced here: 654 us
  blocking collectives  362 us (55%)
  waiting for transfers between devices  130 us (20%)
  local copies, waits for them, and re-layouts  60.6 us (9%)
  other arithmetic  58.7 us (9%)
  between operations  15.6 us (2%)
  matrix products  14 us (2%)
  starting transfers between devices  12.9 us (2%)
    unnamed x1, blocking collectives  280 us
    psum x1, blocking collectives, body(): lax.psum((query_gain_vector, key_gain_vector + lyric_gain_vector), ('song...  82.4 us
    all_gather x1, waiting for transfers between devices, body(): lax.all_gather(lyric_norm.reshape(lyric_local, model_width), 'seq', axis=...  69.1 us
    all_gather x1, waiting for transfers between devices, body(): lax.all_gather(lyric_values[0], 'seq', axis=0, tiled=True)  53.5 us
    unnamed x66, local copies, waits for them, and re-layouts  21.5 us
    scatter-add x1, other arithmetic, body(): lyric_grad_val = jnp.zeros((lyric_total, head_count, head_size), jnp.floa...  20.2 us
    scatter-add x1, other arithmetic, body(): lyric_grad_key = jnp.zeros((lyric_total, head_count, head_size), jnp.floa...  20.2 us
  transfers between devices with their start and end apart: 7, of which 4 were waited for; matrix products, arithmetic and copies ran while one was open for 16% of the time, Pallas kernels for 0%

commit v1 on v0

--- a/solution.py
+++ b/solution.py
@@ -93,7 +93,9 @@
     lyric_norm = lyric_full.astype(jnp.bfloat16)
     lyric_key_all, lyric_val_all = (
         lax.all_gather(lyric_norm.reshape(lyric_local, model_width), "seq", axis=0, tiled=True),
-        lax.all_gather(lyric_values[0], "seq", axis=0, tiled=True),
+        jnp.concatenate(
+            lax.all_to_all(jnp.stack([lyric_values[0]] * lax.axis_size("seq")), "seq", 0, 0), axis=0
+        ),
     )
     lyric_total = lyric_key_all.shape[0]
     lyric_key_all = lyric_key_all.reshape(lyric_total, head_count, head_size)

time: 656 us -> 588 us (0.90)
  waiting for transfers between devices: 130 us -> 47.2 us
  starting transfers between devices: 12.9 us -> 24.6 us
    all_gather x1 -> x0, waiting for transfers between devices: 53.5 us -> none  [body(): lax.all_gather(lyric_values[0], 'seq', axis=0, tiled=True)]
    all_gather x1, waiting for transfers between devices: 69.1 us -> 32.4 us  [body(): lax.all_gather(lyric_norm.reshape(lyric_local, model_width), 'seq', axis=...]
    all_to_all x0 -> x1, starting transfers between devices: none -> 13 us  [body(): lax.all_to_all(jnp.stack([lyric_values[0]] * lax.axis_size('seq')), 'seq'...]
    ppermute x2, waiting for transfers between devices: 5.67 us -> 14.2 us  [extended_2(): lax.ppermute(lax.slice_in_dim(block, 0, width, axis=dim), axis, backward)]
    all_gather x1 -> x0, local copies, waits for them, and re-layouts: 6.94 us -> none  [body(): lax.all_gather(lyric_values[0], 'seq', axis=0, tiled=True)]
    unnamed x66 -> x69, local copies, waits for them, and re-layouts: 21.5 us -> 22.4 us
  transfers between devices with their start and end apart: 7 -> 7, of which waited for: 4 -> 3; matrix products, arithmetic and copies ran while one was open for 16% -> 18% of each run, Pallas kernels for 0% -> 0%
where the time goes in v1:
time: 588 us; the launch traced here: 586 us
  blocking collectives  365 us (62%)
  local copies, waits for them, and re-layouts  60.5 us (10%)
  other arithmetic  58.7 us (10%)
  waiting for transfers between devices  47.2 us (8%)
  starting transfers between devices  24.6 us (4%)
  between operations  15.9 us (3%)
  matrix products  14 us (2%)
    unnamed x1, blocking collectives  279 us
    psum x1, blocking collectives, body(): lax.psum((query_gain_vector, key_gain_vector + lyric_gain_vector), ('song...  85.7 us
    all_gather x1, waiting for transfers between devices, body(): lax.all_gather(lyric_norm.reshape(lyric_local, model_width), 'seq', axis=...  32.4 us
    unnamed x69, local copies, waits for them, and re-layouts  22.4 us
    scatter-add x1, other arithmetic, body(): lyric_grad_val = jnp.zeros((lyric_total, head_count, head_size), jnp.floa...  20.2 us
    scatter-add x1, other arithmetic, body(): lyric_grad_key = jnp.zeros((lyric_total, head_count, head_size), jnp.floa...  20.2 us
    ppermute x2, waiting for transfers between devices, extended_2(): lax.ppermute(lax.slice_in_dim(block, 0, width, axis=dim), axis, backward)  14.2 us
    all_to_all x1, starting transfers between devices, body(): lax.all_to_all(jnp.stack([lyric_values[0]] * lax.axis_size('seq')), 'seq'...  13 us
  transfers between devices with their start and end apart: 7, of which 3 were waited for; matrix products, arithmetic and copies ran while one was open for 18% of the time, Pallas kernels for 0%

profile of v1, /device:TPU:1, one launch (start us, length us, event | category | flops | bytes accessed | tf_op | source)
XLA Modules:
  0.0 586.0 jit_solution(6345696655939693160)
XLA Ops:
  10.3 2.4 stack.11
  12.7 13.0 %all-to-all-start = ((bf16[64,6,2048]{2,1,0:T(8,128)(2,1)}), bf16[64,6,2048]{2,1,0:T(8,128)(2,1)S(1)}, u32[]{:S(2)}, u32[]{:S(2)}) async-start(bf16[64,6,2048]{2,1,0:T(8,128)(2,1)} %stack.11), calls=%async_computation | async-start | bytes 4194304 | tf_op jit(solution)/shard_map/all_to_all | solution.py:97
  31.0 2.4 collective-permute-start.1
  33.4 3.4 collective-permute-start
  42.4 14.2 %collective-permute-done.1 = bf16[2,128,2048]{1,2,0:T(8,128)(2,1)} collective-permute-done((bf16[2,128,2048]{1,2,0:T(8,128)(2,1)}, bf16[2,128,2048]{1,2,0:T(8,128)(2,1)}, u32[]{:S(2)}, u32[]{:S(2)}) %collective-permute-start.1) | collective-permute-done | bytes 1048608 | tf_op jit(solution)/shard_map/ppermute | solution.py:20
  61.2 2.6 copy.80
  63.8 32.4 %all-gather.3.cloned.1.call-done = bf16[64,6,2048]{2,1,0:T(8,128)(2,1)} async-done(((bf16[1,6,2048]{2,1,0:T(8,128)(2,1)}), bf16[64,6,2048]{2,1,0:T(8,128)(2,1)}) %all-gather.3.cloned.1.call-update) | async-done | bytes 1572880 | tf_op jit(solution)/shard_map/all_gather | solution.py:95
  96.3 4.4 reshape.469
  100.6 3.2 gather_fusion.1
  103.8 2.7 reshape_reshape.3
  106.5 3.3 gather_fusion
  114.7 3.1 fusion.56
  117.9 2.4 multiply_reduce_fusion
  127.3 2.1 collective-permute-start.3
  129.4 3.6 collective-permute-start.2
  135.4 20.2 %scatter_fusion = f32[384,16,128]{2,1,0:T(8,128)S(1)} fusion(f32[384,16,128]{2,1,0:T(8,128)S(1)} %broadcast.404.clone, s32[256]{0:T(256)S(1)} %bitcast.227, f32[256,16,128]{2,1,0:T(8,128)} %copy.87), kind=kCustom, calls=%fused_computation.2 | custom fusion | flops 524288 | bytes 6292480 | tf_op jit(solution)/shard_map/scatter-add | solution.py:136
  155.7 3.0 copy.121
  162.8 20.2 %scatter_fusion.1 = f32[384,16,128]{2,1,0:T(8,128)S(1)} fusion(f32[384,16,128]{2,1,0:T(8,128)S(1)} %broadcast.404.clone.1, s32[256]{0:T(256)S(1)} %bitcast.228, f32[256,16,128]{2,1,0:T(8,128)} %copy.88), kind=kCustom, calls=%fused_computation.3 | custom fusion | flops 524288 | bytes 6292480 | tf_op jit(solution)/shard_map/scatter-add | solution.py:141
  183.0 3.1 copy.120
  186.1 279.4 %all-reduce.7 = bf16[384,2048]{1,0:T(8,128)(2,1)} all-reduce(f32[384,2048]{1,0:T(8,128)} %bitcast.203), channel_id=3, replica_groups=mesh['song'=4,'seq'=64] {'seq'}, use_global_device_ids=true, to_apply=%region_11.13.clone | all-reduce | flops 786432 | bytes 4718592
  465.5 4.2 fusion.18
  471.0 2.4 slice.228
  475.5 2.3 fusion.25
  493.5 85.7 %all-reduce.2 = (f32[128]{0:T(128)}, f32[128]{0:T(128)}) all-reduce(f32[128]{0:T(128)S(1)} %get-tuple-element.206, f32[128]{0:T(128)S(1)} %add.202), channel_id=1, replica_groups=mesh['song'=4,'seq'=64] {'song','seq'}, use_global_device_ids=true, to_apply=%region_13.15 | all-reduce | flops 256 | bytes 2048 | tf_op jit(solution)/shard_map/psum | solution.py:195
  (128 shorter events, 54.4 us)
Async XLA Ops:
  7.2 89.1 %all-gather.3.cloned.1.call-start = ((), (), s32[]{:S(2)}) async-start(), calls=%async_computation.1 | async-start | bytes 2129920 | tf_op jit(solution)/shard_map/all_gather | solution.py:95
  10.2 15.5 %copy-start.21 = (bf16[1,128,2048]{2,1,0:T(8,128)(2,1)S(1)}, bf16[1,128,2048]{2,1,0:T(8,128)(2,1)}, u32[]{:S(2)}) copy-start(bf16[1,128,2048]{2,1,0:T(8,128)(2,1)} %param.38) | copy-start | bytes 1572868
  12.7 91.1 %all-to-all-start = ((bf16[64,6,2048]{2,1,0:T(8,128)(2,1)}), bf16[64,6,2048]{2,1,0:T(8,128)(2,1)S(1)}, u32[]{:S(2)}, u32[]{:S(2)}) async-start(bf16[64,6,2048]{2,1,0:T(8,128)(2,1)} %stack.11), calls=%async_computation | async-start | bytes 4194304 | tf_op jit(solution)/shard_map/all_to_all | solution.py:97
  25.7 465.1 %all-reduce.6.cloned.1.call-start = ((), (), s32[]{:S(2)}) async-start(), calls=%async_computation.2 | async-start | bytes 6291456
  26.0 11.6 %copy-start.12 = (bf16[1,128,2048]{1,2,0:T(8,128)(2,1)}, bf16[1,128,2048]{1,2,0:T(8,128)(2,1)S(1)}, u32[]{:S(2)}) copy-start(bf16[1,128,2048]{1,2,0:T(8,128)(2,1)S(1)} %copy.76) | copy-start | bytes 1572868
  26.0 11.4 %copy-start.26 = (s32[1,1,2]{2,1,0:T(1,128)S(1)}, s32[1,1,2]{2,1,0:T(1,128)}, u32[]{:S(2)}) copy-start(s32[1,1,2]{2,1,0:T(1,128)} %param.44) | copy-start | bytes 28
  27.5 10.0 %copy-start.3 = (bf16[1,128,2048]{1,2,0:T(8,128)(2,1)}, bf16[1,128,2048]{1,2,0:T(8,128)(2,1)S(1)}, u32[]{:S(2)}) copy-start(bf16[1,128,2048]{1,2,0:T(8,128)(2,1)S(1)} %copy.75) | copy-start | bytes 1572868
  28.8 12.1 %copy-start.27 = (u32[256]{0:T(256)S(1)}, u32[256]{0:T(256)}, u32[]{:S(2)}) copy-start(u32[256]{0:T(256)} %constant.274) | copy-start | bytes 3076
  30.0 12.4 %copy-start.25 = (f32[128]{0:T(128)S(1)}, f32[128]{0:T(128)}, u32[]{:S(2)}) copy-start(f32[128]{0:T(128)} %param.41) | copy-start | bytes 1540
  31.0 25.6 %collective-permute-start.1 = (bf16[2,128,2048]{1,2,0:T(8,128)(2,1)}, bf16[2,128,2048]{1,2,0:T(8,128)(2,1)}, u32[]{:S(2)}, u32[]{:S(2)}) collective-permute-start(bf16[2,128,2048]{1,2,0:T(8,128)(2,1)} %pad_maximum_fusion.9), channel_id=1, source_target_pairs={{1,0},{2,1},{3,2},{4,3},{5,4},{6,5},{7,6},{8,7},{9,8},{10,9},{11,1... | collective-permute-start | bytes 3145736 | tf_op jit(solution)/shard_map/ppermute | solution.py:20
  33.4 23.9 %collective-permute-start = (bf16[2,128,2048]{1,2,0:T(8,128)(2,1)}, bf16[2,128,2048]{1,2,0:T(8,128)(2,1)}, u32[]{:S(2)}, u32[]{:S(2)}) collective-permute-start(bf16[2,128,2048]{1,2,0:T(8,128)(2,1)} %pad_maximum_fusion.9), channel_id=1, source_target_pairs={{0,1},{1,2},{2,3},{3,4},{4,5},{5,6},{6,7},{7,8},{8,9},{9,10},{10,1... | collective-permute-start | bytes 3145736 | tf_op jit(solution)/shard_map/ppermute | solution.py:17
  40.9 81.3 %copy-start.1 = (f32[1,128,2048]{1,2,0:T(8,128)}, f32[1,128,2048]{1,2,0:T(8,128)S(1)}, u32[]{:S(2)}) copy-start(f32[1,128,2048]{1,2,0:T(8,128)S(1)} %copy.78) | copy-start | bytes 3145732
  106.5 4.9 copy-start.15
  114.7 3.1 copy-start.19
  123.7 9.4 %copy-start = (f32[1,640,16,128]{1,3,2,0:T(8,128)}, f32[1,640,16,128]{1,3,2,0:T(8,128)S(1)}, u32[]{:S(2)}) copy-start(f32[1,640,16,128]{1,3,2,0:T(8,128)S(1)} %get-tuple-element.236) | copy-start | bytes 15728644
  127.3 354.0 %collective-permute-start.3 = (bf16[2,128,2048]{1,2,0:T(8,128)(2,1)}, bf16[2,128,2048]{1,2,0:T(8,128)(2,1)}, u32[]{:S(2)}, u32[]{:S(2)}) collective-permute-start(bf16[2,128,2048]{1,2,0:T(8,128)(2,1)} %get-tuple-element.226), channel_id=1, source_target_pairs={{1,0},{2,1},{3,2},{4,3},{5,4},{6,5},{7,6},{8,7},{9,8},{10,9},{11,1... | collective-permute-start | bytes 3145736 | tf_op jit(solution)/shard_map/ppermute | solution.py:20
  129.4 351.9 %collective-permute-start.2 = (bf16[2,128,2048]{1,2,0:T(8,128)(2,1)}, bf16[2,128,2048]{1,2,0:T(8,128)(2,1)}, u32[]{:S(2)}, u32[]{:S(2)}) collective-permute-start(bf16[2,128,2048]{1,2,0:T(8,128)(2,1)} %get-tuple-element.225), channel_id=1, source_target_pairs={{0,1},{1,2},{2,3},{3,4},{4,5},{5,6},{6,7},{7,8},{8,9},{9,10},{10,1... | collective-permute-start | bytes 3145736 | tf_op jit(solution)/shard_map/ppermute | solution.py:17
  186.1 279.4 %copy-start.2 = (f32[1,128,2048]{1,2,0:T(8,128)S(1)}, f32[1,128,2048]{1,2,0:T(8,128)}, u32[]{:S(2)}) copy-start(f32[1,128,2048]{1,2,0:T(8,128)} %copy-done.1) | copy-start | bytes 3145732
  186.1 279.4 %copy-start.18 = (bf16[384,16,128]{2,0,1:T(8,128)(2,1)S(1)}, bf16[384,16,128]{2,0,1:T(8,128)(2,1)}, u32[]{:S(2)}) copy-start(bf16[384,16,128]{2,0,1:T(8,128)(2,1)} %copy.80) | copy-start | bytes 4718596
  471.0 10.3 %copy-start.4 = (bf16[1,128,2048]{1,2,0:T(8,128)(2,1)S(1)}, bf16[1,128,2048]{1,2,0:T(8,128)(2,1)}, u32[]{:S(2)}) copy-start(bf16[1,128,2048]{1,2,0:T(8,128)(2,1)} %copy-done.3) | copy-start | bytes 1572868
  471.0 10.3 %copy-start.6 = (bf16[1,128,16,128]{1,3,2,0:T(8,128)(2,1)S(1)}, bf16[1,128,16,128]{1,3,2,0:T(8,128)(2,1)}, u32[]{:S(2)}) copy-start(bf16[1,128,16,128]{1,3,2,0:T(8,128)(2,1)} %copy-done.5) | copy-start | bytes 1572868
  484.7 3.3 copy-start.8
  484.8 3.3 copy-start.10
  488.1 3.8 copy-start.23
  (11 other events, 20.7 us)
Sparse Core Ops, SparseCore 0:
  11.3 84.8 all-gather.2
  158.9 194.5 all-reduce.5
